TPU v7x, 32 devices: a whole 2x2x4 slice. The times are simulated.
32 devices in a mesh: blk: 8 (over z, y), col: 4 (over x, core).
Axes of the slice: x: 2, y: 2, z: 4, core: 2. Of those that a mesh axis runs over, the one named last changes fastest.
Arguments:
- amplitudes: float32 [800, 32, 1601], P('col', 'blk'), may hold values from -6 to 6
- integrals: float32 [2, 1024, 20, 1601], P(None, 'blk', 'col'), may hold values from -0.03125 to 0.03125
- block_ids: int32 [20], replicated, may hold values from 0 to 799, as said below
- mirror: int32 [16], replicated, may hold values from 0 to 15, each once
Outputs:
- ladder_residual: float32 [16, 1024], P('col', 'blk')
Inputs may be any that keep to these rules, and one draw needn't show every extreme that they name: `block_ids`: 20 distinct folded block numbers; 0 and 799 are always among them. `mirror`: a permutation of the slab positions.
All inputs are finite; a program needn't handle non-finite values.
Results may differ from a plain program's by a relative error of at most 0.000073.
Values sent between devices are 32-bit elements; how exact they have to be, the bound alone decides.
A program may use at most 64 MiB of HBM per device.

v0:
```python
import jax
import jax.numpy as jnp
from jax import lax
from jax.sharding import PartitionSpec as P


def body(amplitudes, integrals, block_ids, mirror):
    blocks_here = amplitudes.shape[0]
    block_width = amplitudes.shape[2]
    owned_count = integrals.shape[2]
    local_rows = integrals.shape[1]
    block_base = lax.axis_index("col") * blocks_here
    stacked = integrals.reshape(2 * local_rows, owned_count, block_width)
    wanted = block_ids - block_base
    onehot = (wanted[:, None] == jnp.arange(blocks_here, dtype=jnp.int32)[None, :]).astype(
        jnp.float32
    )
    selected = lax.psum_scatter(
        jnp.einsum("kh,hrl->krl", onehot, amplitudes, precision=lax.Precision.HIGHEST),
        "col",
        scatter_dimension=0,
        tiled=True,
    )
    products = jnp.einsum(
        "kcl,wkl->cw",
        lax.all_gather(selected, "blk", axis=1, tiled=True),
        stacked,
        precision=lax.Precision.HIGHEST,
    )
    pair_count = products.shape[0] // 2
    plus_part = products[:, :local_rows]
    minus_part = products[:, local_rows:]
    direct = 0.5 * (
        plus_part[:pair_count]
        + minus_part[:pair_count]
        + plus_part[pair_count:]
        - minus_part[pair_count:]
    )
    swapped = 0.5 * (
        plus_part[:pair_count]
        - minus_part[:pair_count]
        + plus_part[pair_count:]
        + minus_part[pair_count:]
    )
    direct_sum, swapped_sum = (
        lax.psum_scatter(direct, "col", scatter_dimension=0, tiled=True),
        lax.psum_scatter(swapped, "col", scatter_dimension=0, tiled=True),
    )
    swapped_all = lax.all_gather(swapped_sum, "col", axis=0, tiled=True)
    own_pairs = direct_sum.shape[0]
    targets = lax.dynamic_slice_in_dim(mirror, lax.axis_index("col") * own_pairs, own_pairs)
    pick = (targets[:, None] == jnp.arange(pair_count, dtype=jnp.int32)[None, :]).astype(
        jnp.float32
    )
    return direct_sum + jnp.dot(pick, swapped_all, precision=lax.Precision.HIGHEST)


def solution(mesh):
    in_specs = (P("col", "blk", None), P(None, "blk", "col", None), P(), P())
    out_specs = P("col", "blk")
    return jax.shard_map(body, mesh=mesh, in_specs=in_specs, out_specs=out_specs, check_vma=False)
```

profile of v0, /device:TPU:0, one launch (start us, length us, event | category | flops | bytes accessed | tf_op | source)
XLA Modules:
  0.0 118.5 jit_solution(15536446643626224223)
XLA Ops:
  6.5 0.0 copy-start.1
  6.5 0.0 all-reduce.6.cloned.1.call-start
  6.5 0.7 broadcast_subtract_fusion
  7.2 4.3 %fusion = f32[20,4,1601]{2,0,1:T(8,128)S(1)} fusion(f32[200,4,1601]{2,1,0:T(4,128)} %param.4, s32[20]{0:T(128)S(1)} %broadcast_subtract_fusion), kind=kOutput, calls=%fused_computation | convolution fusion | flops 307396000 | bytes 5635600 | tf_op jit(solution)/shard_map/kh,hrl->krl/dot_general | solution.py:19
  11.6 1.0 copy.8
  12.6 0.0 all-reduce.6.cloned.1.call-update
  12.6 0.0 copy-done.1
  12.6 0.6 dynamic-slice
  14.5 0.0 copy-start
  14.5 10.6 %reshape.5 = f32[256,5,1601]{0,2,1:T(8,128)} reshape(f32[2,128,5,1601]{1,0,3,2:T(2,128)} %param.5) | data formatting | bytes 16394240 | tf_op jit(solution)/shard_map/reshape | solution.py:13
  25.1 0.0 copy-done
  25.1 0.1 dynamic_slice.3
  25.2 23.6 %all-reduce.6.cloned.1.call-done = f32[20,4,1601]{2,1,0:T(4,128)} async-done(((f32[20,4,1601]{2,1,0:T(4,128)}), f32[20,4,1601]{2,1,0:T(4,128)}) %all-reduce.6.cloned.1.call-update) | async-done | bytes 512336
  48.8 0.9 constant_dynamic-slice_fusion
  49.7 38.5 %all_gather.6 = f32[5,32,1601]{2,0,1:T(8,128)S(1)} all-gather(f32[5,4,1601]{2,0,1:T(8,128)S(1)} %copy.5), channel_id=1, replica_groups=mesh['blk'=8,'col'=4] {'blk'}, dimensions={1}, use_global_device_ids=true | all-gather | bytes 1152720 | tf_op jit(solution)/shard_map/all_gather | solution.py:26
  88.3 7.3 %convolution_bitcast_fusion = f32[32,256]{1,0:T(8,128)S(1)} fusion(f32[256,5,1601]{0,2,1:T(8,128)} %reshape.5, f32[5,32,1601]{2,0,1:T(8,128)S(1)} %all_gather.6), kind=kOutput, calls=%fused_computation.2 | convolution fusion | flops 786923520 | bytes 9254528 | tf_op jit(solution)/shard_map/kcl,wkl->cw/dot_general | solution.py:24
  95.6 10.1 %all-reduce.3 = (f32[16,128]{1,0:T(8,128)S(1)}, f32[16,128]{1,0:T(8,128)S(1)}) all-reduce(f32[16,128]{1,0:T(8,128)S(1)} %get-tuple-element.8, f32[16,128]{1,0:T(8,128)S(1)} %get-tuple-element.7), channel_id=4, replica_groups=mesh['blk'=8,'col'=4] {'col'}, use_global_device_ids=true, to_apply=%region_2.0.clone | all-reduce | flops 4096 | bytes 32768
  105.7 5.2 %all-gather = f32[4,4,128]{2,1,0:T(4,128)S(1)} all-gather(f32[1,4,128]{2,1,0:T(4,128)S(1)} %dynamic-slice_bitcast_fusion), channel_id=1, replica_groups=mesh['blk'=8,'col'=4] {'col'}, dimensions={0}, use_global_device_ids=true | all-gather | bytes 10240 | tf_op jit(solution)/shard_map/all_gather | solution.py:49
  110.9 0.8 convolution_add_fusion
  (3 shorter events, 0.0 us)
Async XLA Ops:
  6.5 6.1 %copy-start.1 = (u32[32]{0:T(128)S(1)}, u32[32]{0:T(128)}, u32[]{:S(2)}) copy-start(u32[32]{0:T(128)} %constant.18) | copy-start | bytes 388
  6.5 42.3 %all-reduce.6.cloned.1.call-start = ((), (), s32[]{:S(2)}) async-start(), calls=%async_computation | async-start | bytes 1064960
  14.5 10.7 %copy-start = (s32[16]{0:T(128)S(1)}, s32[16]{0:T(128)}, u32[]{:S(2)}) copy-start(s32[16]{0:T(128)} %param.7) | copy-start | bytes 196
Sparse Core Ops, SparseCore 0:
  12.7 36.0 all-reduce.5
where the time goes:
time: 119 us
  blocking collectives  53.9 us (45%)
  waiting for transfers between devices  23.6 us (20%)
  between operations  14.7 us (12%)
  local copies, waits for them, and re-layouts  13.3 us (11%)
  matrix products  12.4 us (10%)
    all_gather x1, blocking collectives, body(): lax.all_gather(selected, 'blk', axis=1, tiled=True)  38.5 us
    unnamed x2, waiting for transfers between devices  23.6 us
    reshape x1, local copies, waits for them, and re-layouts, body(): stacked = integrals.reshape(2 * local_rows, owned_count, block_width)  10.6 us
    unnamed x1, blocking collectives  10.1 us
    dot_general x1, matrix products, body(): jnp.einsum('kcl,wkl->cw', lax.all_gather(selected, 'blk', axis=1, tiled=T...  7.29 us
    all_gather x1, blocking collectives, body(): swapped_all = lax.all_gather(swapped_sum, 'col', axis=0, tiled=True)  5.19 us
    dot_general x1, matrix products, body(): jnp.einsum('kh,hrl->krl', onehot, amplitudes, precision=lax.Precision.HIG...  4.35 us
  transfers between devices with their start and end apart: 1, of which 1 were waited for; matrix products, arithmetic and copies ran while one was open for 10% of the time, Pallas kernels for 0%

commit v1 on v0

--- a/solution.py
+++ b/solution.py
@@ -23,7 +23,7 @@
     )
     products = jnp.einsum(
         "kcl,wkl->cw",
-        lax.all_gather(selected, "blk", axis=1, tiled=True),
+        jnp.concatenate(lax.all_gather(selected, "blk"), axis=1),
         stacked,
         precision=lax.Precision.HIGHEST,
     )

time: 119 us -> 115 us (0.966)
  blocking collectives: 53.9 us -> 49.5 us
    all_gather x1, blocking collectives: 38.5 us -> 33.8 us  [body(): lax.all_gather(selected, 'blk')]
where the time goes in v1:
time: 115 us; the launch traced here: 114 us
  blocking collectives  49.5 us (43%)
  waiting for transfers between devices  23.6 us (21%)
  between operations  14.7 us (13%)
  local copies, waits for them, and re-layouts  13.7 us (12%)
  matrix products  12.2 us (11%)
    all_gather x1, blocking collectives, body(): lax.all_gather(selected, 'blk')  33.8 us
    unnamed x2, waiting for transfers between devices  23.6 us
    reshape x1, local copies, waits for them, and re-layouts, body(): stacked = integrals.reshape(2 * local_rows, owned_count, block_width)  10.6 us
    unnamed x1, blocking collectives  10.5 us
    dot_general x1, matrix products, body(): jnp.einsum('kcl,wkl->cw', jnp.concatenate(lax.all_gather(selected, 'blk')...  7.1 us
    all_gather x1, blocking collectives, body(): swapped_all = lax.all_gather(swapped_sum, 'col', axis=0, tiled=True)  5.19 us
    dot_general x1, matrix products, body(): jnp.einsum('kh,hrl->krl', onehot, amplitudes, precision=lax.Precision.HIG...  4.35 us
  transfers between devices with their start and end apart: 1, of which 1 were waited for; matrix products, arithmetic and copies ran while one was open for 10% of the time, Pallas kernels for 0%

profile of v1, /device:TPU:0, one launch (start us, length us, event | category | flops | bytes accessed | tf_op | source)
XLA Modules:
  0.0 114.4 jit_solution(7860244013937841792)
XLA Ops:
  6.5 0.0 copy-start.1
  6.5 0.0 all-reduce.6.cloned.1.call-start
  6.5 0.7 broadcast_subtract_fusion
  7.2 4.3 %fusion = f32[20,4,1601]{2,0,1:T(8,128)S(1)} fusion(f32[200,4,1601]{2,1,0:T(4,128)} %param.4, s32[20]{0:T(128)S(1)} %broadcast_subtract_fusion), kind=kOutput, calls=%fused_computation | convolution fusion | flops 307396000 | bytes 5635600 | tf_op jit(solution)/shard_map/kh,hrl->krl/dot_general | solution.py:19
  11.6 1.0 copy.11
  12.6 0.0 all-reduce.6.cloned.1.call-update
  12.6 0.0 copy-done.1
  12.6 0.6 dynamic-slice
  14.5 0.0 copy-start
  14.5 10.6 %reshape.13 = f32[256,5,1601]{0,2,1:T(8,128)} reshape(f32[2,128,5,1601]{1,0,3,2:T(2,128)} %param.5) | data formatting | bytes 16394240 | tf_op jit(solution)/shard_map/reshape | solution.py:13
  25.1 0.0 copy-done
  25.1 0.1 dynamic_slice.3
  25.2 23.6 %all-reduce.6.cloned.1.call-done = f32[20,4,1601]{2,1,0:T(4,128)} async-done(((f32[20,4,1601]{2,1,0:T(4,128)}), f32[20,4,1601]{2,1,0:T(4,128)}) %all-reduce.6.cloned.1.call-update) | async-done | bytes 512336
  48.8 0.9 constant_dynamic-slice_fusion
  49.7 33.8 %all-gather = f32[40,4,1601]{2,1,0:T(4,128)S(1)} all-gather(f32[5,4,1601]{2,1,0:T(4,128)S(1)} %constant_dynamic-slice_fusion), channel_id=2, replica_groups=mesh['blk'=8,'col'=4] {'blk'}, dimensions={0}, use_global_device_ids=true | all-gather | bytes 1152720 | tf_op jit(solution)/shard_map/all_gather | solution.py:26
  83.5 0.1 copy.12
  83.6 0.4 reshape.12
  84.0 7.1 %convolution_bitcast_fusion = f32[32,256]{1,0:T(8,128)S(1)} fusion(f32[5,32,1601]{2,1,0:T(8,128)S(1)} %reshape.12, f32[256,5,1601]{0,2,1:T(8,128)} %reshape.13), kind=kOutput, calls=%fused_computation.2 | convolution fusion | flops 786923520 | bytes 9254528 | tf_op jit(solution)/shard_map/kcl,wkl->cw/dot_general | solution.py:24
  91.1 10.5 %all-reduce.3 = (f32[16,128]{1,0:T(8,128)S(1)}, f32[16,128]{1,0:T(8,128)S(1)}) all-reduce(f32[16,128]{1,0:T(8,128)S(1)} %get-tuple-element.8, f32[16,128]{1,0:T(8,128)S(1)} %get-tuple-element.7), channel_id=5, replica_groups=mesh['blk'=8,'col'=4] {'col'}, use_global_device_ids=true, to_apply=%region_2.0.clone | all-reduce | flops 4096 | bytes 32768
  101.6 5.2 %all-gather.1 = f32[4,4,128]{2,1,0:T(4,128)S(1)} all-gather(f32[1,4,128]{2,1,0:T(4,128)S(1)} %dynamic-slice_bitcast_fusion), channel_id=1, replica_groups=mesh['blk'=8,'col'=4] {'col'}, dimensions={0}, use_global_device_ids=true | all-gather | bytes 10240 | tf_op jit(solution)/shard_map/all_gather | solution.py:49
  106.8 0.8 convolution_add_fusion
  (2 shorter events, 0.0 us)
Async XLA Ops:
  6.5 6.1 %copy-start.1 = (u32[32]{0:T(128)S(1)}, u32[32]{0:T(128)}, u32[]{:S(2)}) copy-start(u32[32]{0:T(128)} %constant.18) | copy-start | bytes 388
  6.5 42.3 %all-reduce.6.cloned.1.call-start = ((), (), s32[]{:S(2)}) async-start(), calls=%async_computation | async-start | bytes 1064960
  14.5 10.7 %copy-start = (s32[16]{0:T(128)S(1)}, s32[16]{0:T(128)}, u32[]{:S(2)}) copy-start(s32[16]{0:T(128)} %param.7) | copy-start | bytes 196
Sparse Core Ops, SparseCore 0:
  12.7 36.0 all-reduce.5
